TPU v7x, 32 devices: a whole 2x2x4 slice. The times are simulated.
32 devices in a mesh: band: 2 (over x), col: 16 (over z, y, core).
Axes of the slice: x: 2, y: 2, z: 4, core: 2. Of those that a mesh axis runs over, the one named last changes fastest.
Arguments:
- fields: bfloat16 [4, 80, 16, 2048], P(None, None, 'band', 'col'), may hold values from -6 to 6
- inverse: bfloat16 [4, 80, 80], replicated, may hold values from -1 to 2
- block_costs: int32 [16, 16], P('col', 'band'), may hold values from 1 to 8, as said below
- row_length: int32 [16], P('band'), may hold values from 1025 to 2048
Outputs:
- spectra: float32 [320, 16, 2, 512], P('col', None, None, 'band')
Inputs may be any that keep to these rules, and one draw needn't show every extreme that they name: `block_costs`: at least one block takes 8 substeps and at least one takes 1.
All inputs are finite; a program needn't handle non-finite values.
Results may differ from a plain program's by a relative error of at most 0.0042.
Values may be sent and summed in bfloat16 or wider, within the bound.
A program may use at most 64 MiB of HBM per device.

v0:
```python
import math

import jax
import jax.numpy as jnp
from jax import lax
from jax.sharding import PartitionSpec as P

group_width = 4


def relax(blocks, counts, inverse):
    group_total = blocks.shape[2] // group_width

    def one_group(group_index, result):
        offset_start = group_index * group_width
        block_set = lax.dynamic_slice_in_dim(blocks, offset_start, group_width, 2)
        steps_here = lax.dynamic_slice_in_dim(counts, offset_start, group_width, 0)

        def sweep(sweep_index, block_state):
            applied = jnp.einsum(
                "fkl,flgb->fkgb", inverse, block_state, preferred_element_type=jnp.float32
            ).astype(jnp.bfloat16)
            return jnp.where((sweep_index < steps_here)[None, None, :, None], applied, block_state)

        block_set = lax.fori_loop(jnp.int32(0), jnp.max(steps_here), sweep, block_set)
        return lax.dynamic_update_slice_in_dim(result, block_set, offset_start, 2)

    return lax.fori_loop(0, group_total, one_group, blocks)


def tendency_of(relaxed, initial):
    return (relaxed.astype(jnp.float32) - initial.astype(jnp.float32)).astype(jnp.bfloat16)


def apply_tendency(initial, tendency):
    tendency = lax.optimization_barrier(tendency)
    return (initial.astype(jnp.float32) + tendency.astype(jnp.float32)).astype(jnp.bfloat16)


def mask_rows(values_in, lengths, first_longitude):
    block_width = values_in.shape[3]
    longitude = first_longitude + jnp.arange(block_width, dtype=jnp.int32)
    keep_mask = longitude[None, :] < lengths[:, None]
    return jnp.where(keep_mask[None, None], values_in, jnp.zeros_like(values_in))


def transform(row_piece, wave_total):
    group_count = lax.axis_size("col")
    length_all = row_piece.shape[-1]
    block_width = length_all // group_count
    level_count = row_piece.shape[0]
    piece_rows = row_piece.shape[1]
    values_f32 = row_piece.astype(jnp.float32).reshape(
        level_count, piece_rows, group_count, block_width
    )
    group_ids = jnp.arange(group_count, dtype=jnp.int32)
    angle_one = (group_ids[:, None] * group_ids[None, :] % group_count).astype(jnp.float32) * (
        2.0 * math.pi / group_count
    )
    table_one = jnp.stack([jnp.cos(angle_one), -jnp.sin(angle_one)], axis=0)
    section_one = jnp.einsum(
        "icm,prcb->iprmb", table_one, values_f32, precision=lax.Precision.HIGHEST
    )
    lane_ids = jnp.arange(block_width, dtype=jnp.int32)
    angle_twist = (group_ids[:, None] * lane_ids[None, :] % length_all).astype(jnp.float32) * (
        2.0 * math.pi / length_all
    )
    cos_twist = jnp.cos(angle_twist)
    sin_twist = jnp.sin(angle_twist)
    real_part = section_one[0] * cos_twist + section_one[1] * sin_twist
    imaginary = section_one[1] * cos_twist - section_one[0] * sin_twist
    twisted = jnp.stack([real_part, imaginary], axis=0)
    wave_ids = jnp.arange(wave_total, dtype=jnp.int32)
    angle_two = (lane_ids[:, None] * wave_ids[None, :] % block_width).astype(jnp.float32) * (
        2.0 * math.pi / block_width
    )
    cos_two = jnp.cos(angle_two)
    sin_two = jnp.sin(angle_two)
    table_two = jnp.stack(
        [jnp.stack([cos_two, -sin_two], axis=1), jnp.stack([sin_two, cos_two], axis=1)], axis=0
    )
    section_two = jnp.einsum(
        "iprmb,iboq->proqm", twisted, table_two, precision=lax.Precision.HIGHEST
    )
    return section_two.reshape(level_count, piece_rows, 2, wave_total * group_count) / math.sqrt(
        length_all
    )


def whole_transform(row_piece):
    quarter = row_piece.shape[-1] // lax.axis_size("col") // 4
    return transform(row_piece, quarter)


def shards(fields, inverse, block_costs, row_length):
    field_levels = fields.shape[0] * fields.shape[1]
    row_count = fields.shape[2]
    block_width = fields.shape[3]
    own_cost = block_costs[0]
    first_longitude = lax.axis_index("col") * block_width
    relaxed = relax(fields, own_cost, inverse)
    updated = apply_tendency(fields, tendency_of(relaxed, fields))
    masked = mask_rows(updated, row_length, first_longitude)
    flat_blocks = masked.reshape(field_levels, row_count, block_width)
    rows_fourier = whole_transform(
        lax.all_to_all(flat_blocks, "col", split_axis=0, concat_axis=2, tiled=True)
    )
    return lax.all_to_all(rows_fourier, "band", split_axis=3, concat_axis=1, tiled=True)


def solution(mesh):
    return jax.shard_map(
        shards,
        mesh=mesh,
        in_specs=(P(None, None, "band", "col"), P(), P("col", "band"), P("band")),
        out_specs=P("col", None, None, "band"),
        check_vma=False,
    )
```

profile of v0, /device:TPU:0, one launch (start us, length us, event | category | flops | bytes accessed | tf_op | source)
XLA Modules:
  0.0 90.1 jit_solution(12108789757390469402)
XLA Ops:
  0.0 1.2 %copy.84 = bf16[4,80,8,128]{3,2,1,0:T(8,128)(2,1)S(1)} copy(bf16[4,80,8,128]{3,2,1,0:T(8,128)(2,1)} %param.8) | data formatting | bytes 1310720
  1.3 12.7 %while.36 = (s32[]{:T(128)}, bf16[4,80,8,128]{3,2,1,0:T(8,128)(2,1)S(1)}, bf16[4,80,8,128]{3,2,1,0:T(8,128)(2,1)S(1)}, s32[8]{0:T(128)S(1)}, bf16[4,80,80]{2,1,0...) while((s32[]{:T(128)}, ...), condition=%wide.region_4.5_spmd, body=%wide.region_0.4_spmd.sunk | while | flops 26542092 | bytes 3328356 | solution.py:28
  1.3 0.8 fusion.49
  2.3 8.5 %while.37 = (s32[]{:T(128)}, bf16[4,80,4,128]{3,1,2,0:T(8,128)(2,1)S(1)}, s32[]{:T(128)}, s32[4]{0:T(128)S(1)}, bf16[4,80,80]{2,1,0:T(8,128)(2,1)S(1)}, /*index=5*/s32[]{:T(128)}) while((s32[]{:T(128)}, bf16[4,80,4,128]{3,1,2,0:T(8,128)(2,1)S(1)}, s32[]{:T(128)}, s32[4]{0:T(128)S(1)}, bf16[4,80,80]{2,1,0:T(8,128)(2,1)S(1)}, ...), condition=%wide.region_3.3_spmd, body=%wide.region_2.2_spmd.sunk | while | flops 26542084 | bytes 1362017 | solution.py:25
  3.0 0.2 fusion.52
  4.0 0.2 fusion.52
  5.0 0.2 fusion.52
  6.0 0.2 fusion.52
  6.9 0.2 fusion.52
  7.9 0.2 fusion.52
  8.9 0.2 fusion.52
  9.9 0.2 fusion.52
  10.8 0.2 copy_dynamic-update-slice_fusion.2
  11.1 0.8 fusion.49
  12.1 1.7 %while.37 = (s32[]{:T(128)}, bf16[4,80,4,128]{3,1,2,0:T(8,128)(2,1)S(1)}, s32[]{:T(128)}, s32[4]{0:T(128)S(1)}, bf16[4,80,80]{2,1,0:T(8,128)(2,1)S(1)}, /*index=5*/s32[]{:T(128)}) while((s32[]{:T(128)}, bf16[4,80,4,128]{3,1,2,0:T(8,128)(2,1)S(1)}, s32[]{:T(128)}, s32[4]{0:T(128)S(1)}, bf16[4,80,80]{2,1,0:T(8,128)(2,1)S(1)}, ...), condition=%wide.region_3.3_spmd, body=%wide.region_2.2_spmd.sunk | while | flops 26542084 | bytes 1362017 | solution.py:25
  13.7 0.2 copy_dynamic-update-slice_fusion.2
  14.2 0.5 copy-done.3
  14.7 1.1 %fusion.10 = bf16[4,80,8,128]{3,2,1,0:T(8,128)(2,1)} fusion(bf16[4,80,8,128]{3,2,1,0:T(8,128)(2,1)S(1)} %fusion.8, bf16[4,80,8,128]{3,2,1,0:T(8,128)(2,1)S(1)} %get-tuple-element.315, pred[8,128]{1,0:T(8,128)(4,1)S(1)} %broadcast_compare_fusion.1), kind=kLoop, calls=%fused_computation.19 | loop fusion | flops 1638400 | bytes 1967104 | tf_op jit(solution)/shard_map/jit(_where)/select_n | solution.py:44
  15.8 13.3 %all-to-all-start = ((bf16[320,8,128]{2,1,0:T(8,128)(2,1)}), bf16[320,8,128]{2,1,0:T(8,128)(2,1)S(1)}, u32[]{:S(2)}, u32[]{:S(2)}) async-start(bf16[320,8,128]{2,1,0:T(8,128)(2,1)} %bitcast.8), calls=%async_computation | async-start | bytes 1310720 | tf_op jit(solution)/shard_map/all_to_all | solution.py:106
  29.4 16.2 %all-to-all-done = bf16[320,8,128]{2,1,0:T(8,128)(2,1)S(1)} async-done(((bf16[320,8,128]{2,1,0:T(8,128)(2,1)}), bf16[320,8,128]{2,1,0:T(8,128)(2,1)S(1)}, u32[]{:S(2)}, u32[]{:S(2)}) %all-to-all-start) | async-done | bytes 655392 | tf_op jit(solution)/shard_map/all_to_all | solution.py:106
  45.6 1.2 %convolution_bitcast_fusion = f32[2,20,8,16,128]{4,3,0,2,1:T(8,128)S(1)} fusion(bf16[16,20,8,128]{3,2,1,0:T(8,128)(2,1)S(1)} %bitcast.62, f32[1,16,16]{1,2,0:T(8,128)S(1)} %get-tuple-element.179, f32[1,16,16]{1,2,0:T(8,128)S(1)} %get-tuple-element.180), kind=kOutput, calls=%fused_computation.12 | convolution fusion | flops 125829632 | bytes 3278848 | tf_op jit(solution)/shard_map/icm,prcb->iprmb/dot_general | solution.py:61
  46.8 0.4 multiply_add_fusion
  47.2 0.2 pad_maximum_fusion
  47.5 3.6 %fusion.2 = f32[20,8,2,32,16]{3,0,4,1,2:T(8,128)S(1)} fusion(f32[2,20,8,16,128]{4,3,0,2,1:T(8,128)S(1)} %pad_maximum_fusion, f32[1,128,2,32]{1,3,0,2:T(8,128)S(1)} %get-tuple-element.178, f32[1,128,2,32]{1,3,0,2:T(8,128)S(1)} %get-tuple-element.177), kind=kOutput, calls=%fused_computation.7 | convolution fusion | flops 503496704 | bytes 3342336 | tf_op jit(solution)/shard_map/iprmb,iboq->proqm/dot_general | solution.py:82
  51.1 5.2 %copy.53 = f32[20,8,2,32,16]{0,1,2,4,3:T(8,128)} copy(f32[20,8,2,32,16]{3,0,4,1,2:T(8,128)S(1)} %fusion.2) | data formatting | bytes 1310720 | tf_op jit(solution)/shard_map/div | solution.py:85
  56.3 6.0 %reshape.230 = f32[2,1,81920]{2,1,0:T(1,128)S(1)} reshape(f32[512,2,8,20]{3,2,1,0:T(8,128)} %bitcast.58) | data formatting | bytes 1310720
  62.3 12.4 %all_to_all.33 = f32[2,1,81920]{2,1,0:T(1,128)S(1)} all-to-all(f32[2,1,81920]{2,1,0:T(1,128)S(1)} %reshape.230), channel_id=1, replica_groups=mesh['band'=2,'col'=16] {'band'}, dimensions={0} | all-to-all | bytes 1310720 | tf_op jit(solution)/shard_map/all_to_all | solution.py:108
  74.8 0.5 broadcast.296
  75.3 2.7 %reduce = f32[2,81920]{1,0:T(2,128)S(1)} reduce(f32[2,1,81920]{2,1,0:T(1,128)S(1)} %all_to_all.33, f32[]{:T(128)} %broadcast.296), dimensions={1}, to_apply=%all_to_all.27.reduce_sub_computation | reduce | bytes 1310724 | tf_op jit(solution)/shard_map/all_to_all | solution.py:108
  78.0 6.9 %reshape.231 = f32[512,2,8,20]{3,2,1,0:T(8,128)} reshape(f32[2,81920]{1,0:T(2,128)S(1)} %reduce) | data formatting | bytes 1310720
  84.9 3.7 %copy.54 = f32[20,8,2,2,256]{4,3,1,2,0:T(2,128)S(1)} copy(f32[20,8,2,2,256]{0,1,2,4,3:T(8,128)} %bitcast.59) | data formatting | bytes 1310720 | tf_op jit(solution)/shard_map/all_to_all | solution.py:108
  88.7 1.3 %copy.47 = f32[20,16,2,256]{3,2,1,0:T(2,128)} copy(f32[20,16,2,256]{3,1,2,0:T(8,128)S(1)} %bitcast.61) | data formatting | bytes 1310720 | tf_op jit(solution)/shard_map/all_to_all | solution.py:108
  (39 shorter events, 1.7 us)
Async XLA Ops:
  0.0 1.3 %copy-start.1 = (bf16[4,80,8,128]{3,2,1,0:T(8,128)(2,1)S(1)}, bf16[4,80,8,128]{3,2,1,0:T(8,128)(2,1)}, u32[]{:S(2)}) copy-start(bf16[4,80,8,128]{3,2,1,0:T(8,128)(2,1)} %param.8) | copy-start | bytes 1966084
  0.0 1.3 %copy-start.2 = (s32[1,8]{1,0:T(1,128)S(1)}, s32[1,8]{1,0:T(1,128)}, u32[]{:S(2)}) copy-start(s32[1,8]{1,0:T(1,128)} %param.10) | copy-start | bytes 100
  0.0 1.3 %copy-start = (bf16[4,80,80]{2,1,0:T(8,128)(2,1)S(1)}, bf16[4,80,80]{2,1,0:T(8,128)(2,1)}, u32[]{:S(2)}) copy-start(bf16[4,80,80]{2,1,0:T(8,128)(2,1)} %param.9) | copy-start | bytes 153604
  14.0 0.7 copy-start.3
  15.8 29.9 %all-to-all-start = ((bf16[320,8,128]{2,1,0:T(8,128)(2,1)}), bf16[320,8,128]{2,1,0:T(8,128)(2,1)S(1)}, u32[]{:S(2)}, u32[]{:S(2)}) async-start(bf16[320,8,128]{2,1,0:T(8,128)(2,1)} %bitcast.8), calls=%async_computation | async-start | bytes 1310720 | tf_op jit(solution)/shard_map/all_to_all | solution.py:106
where the time goes:
time: 90.5 us; the launch traced here: 90.1 us
  local copies, waits for them, and re-layouts  26.6 us (29%)
  waiting for transfers between devices  16.2 us (18%)
  starting transfers between devices  13.3 us (15%)
  blocking collectives  12.4 us (14%)
  loops' own time  7.9 us (9%)
  matrix products  6.9 us (8%)
  other arithmetic  6.54 us (7%)
    all_to_all x1, waiting for transfers between devices, shards(): lax.all_to_all(flat_blocks, 'col', split_axis=0, concat_axis=2, tiled=True)  16.2 us
    unnamed x11, local copies, waits for them, and re-layouts  14.7 us
    all_to_all x1, starting transfers between devices, shards(): lax.all_to_all(flat_blocks, 'col', split_axis=0, concat_axis=2, tiled=True)  13.3 us
    all_to_all x1, blocking collectives, shards(): lax.all_to_all(rows_fourier, 'band', split_axis=3, concat_axis=1, tiled=T...  12.4 us
    another operation x2, loops' own time, one_group(): lax.fori_loop(jnp.int32(0), jnp.max(steps_here), sweep, block_set)  7.82 us
    all_to_all x4, local copies, waits for them, and re-layouts, shards(): lax.all_to_all(rows_fourier, 'band', split_axis=3, concat_axis=1, tiled=T...  5.65 us
    div x1, local copies, waits for them, and re-layouts, transform(): section_two.reshape(level_count, piece_rows, 2, wave_total * group_count)  5.19 us
    dot_general x1, matrix products, transform(): jnp.einsum('iprmb,iboq->proqm', twisted, table_two, precision=lax.Precisi...  3.63 us
  transfers between devices with their start and end apart: 1, of which 1 were waited for; matrix products, arithmetic and copies ran while one was open for 0% of the time, Pallas kernels for 0%

commit v1 on v0

v1 whole, which is shorter than its diff:
```python
import functools
import math

import jax
import jax.numpy as jnp
import numpy as np
from jax import lax
from jax.experimental import pallas as pl
from jax.experimental.pallas import tpu as pltpu
from jax.sharding import PartitionSpec as P

sweep_total = 8
MESH = pl.DeviceIdType.MESH


def flip(position, step, total):
    result, bit = 0, 1
    while bit < total:
        result = result + bit * (((position // bit) + (step // bit)) % 2)
        bit *= 2
    return result


def relax_kernel(cost_ref, length_ref, fields_ref, inverse_ref, out_ref, start_ref, state_ref, turn_ref):
    field_total, level_total, row_total, width = fields_ref.shape
    first = lax.axis_index("col") * width
    for f in range(field_total):
        turn_ref[f] = fields_ref[f].astype(jnp.float32).reshape(level_total * row_total, width)
    for f in range(field_total):
        for r in range(row_total):
            piece = turn_ref[f, pl.ds(r, level_total, stride=row_total), :].astype(jnp.bfloat16)
            start_ref[f, :, r * width : (r + 1) * width] = piece
            state_ref[f, :, r * width : (r + 1) * width] = piece
    costs = jnp.concatenate(
        [jnp.full((1, width), cost_ref[0, r], jnp.int32) for r in range(row_total)], axis=1
    )

    def sweep(s, carry):
        active = costs > s
        for f in range(field_total):
            before = state_ref[f]
            applied = jnp.dot(inverse_ref[f], before, preferred_element_type=jnp.float32)
            state_ref[f] = jnp.where(active, applied, before.astype(jnp.float32)).astype(jnp.bfloat16)
        return carry

    lax.fori_loop(0, sweep_total, sweep, 0)
    longitude = first + lax.broadcasted_iota(jnp.int32, (1, width), 1)
    for f in range(field_total):
        for r in range(row_total):
            initial = start_ref[f, :, r * width : (r + 1) * width].astype(jnp.float32)
            relaxed = state_ref[f, :, r * width : (r + 1) * width].astype(jnp.float32)
            tendency = (relaxed - initial).astype(jnp.bfloat16)
            updated = (initial + tendency.astype(jnp.float32)).astype(jnp.bfloat16)
            keep = longitude < length_ref[r]
            turn_ref[f, pl.ds(r, level_total, stride=row_total), :] = jnp.where(
                keep, updated.astype(jnp.float32), 0.0
            )
    for f in range(field_total):
        out_ref[f] = turn_ref[f].reshape(level_total, row_total, width).astype(jnp.bfloat16)


def fourier_kernel(
    col_total, band_total, blocks_ref, base_ref, phase_ref, out_ref,
    landed, total, outgoing, incoming, base_buf, send_sem, recv_sem, band_send, band_recv, base_sem,
):
    me, band = lax.axis_index("col"), lax.axis_index("band")
    level_total, row_total, width = landed.shape[1:]
    piece_width = total.shape[2]
    barrier = pltpu.get_barrier_semaphore()
    base_copy = pltpu.make_async_copy(base_ref, base_buf, base_sem)
    base_copy.start()

    def greet(t, carry):
        pl.semaphore_signal(
            barrier, inc=1, device_id={"col": flip(me, t, col_total)}, device_id_type=MESH
        )
        return carry

    lax.fori_loop(1, col_total, greet, 0)
    for j in range(1, band_total):
        pl.semaphore_signal(
            barrier, inc=1, device_id={"band": (band + j) % band_total}, device_id_type=MESH
        )
    pl.semaphore_wait(barrier, col_total - 1 + band_total - 1)

    def block_copy(t):
        peer = flip(me, t, col_total)
        return pltpu.make_async_remote_copy(
            src_ref=blocks_ref.at[peer],
            dst_ref=landed.at[me],
            send_sem=send_sem.at[peer],
            recv_sem=recv_sem.at[me],
            device_id={"col": peer},
            device_id_type=MESH,
        )

    def arrival(t):
        peer = flip(me, t, col_total)
        return pltpu.make_async_remote_copy(
            src_ref=blocks_ref.at[peer],
            dst_ref=landed.at[peer],
            send_sem=send_sem.at[peer],
            recv_sem=recv_sem.at[peer],
            device_id={"col": peer},
            device_id_type=MESH,
        )

    def send(t, carry):
        block_copy(col_total - t).start()
        return carry

    lax.fori_loop(1, col_total, send, 0)
    base_copy.wait()

    def accumulate(block, source, first):
        rows = block.astype(jnp.float32).reshape(level_total * row_total, width).astype(jnp.bfloat16)
        for j in range(band_total):
            lanes = slice(j * piece_width, (j + 1) * piece_width)
            table = (
                base_buf[0, :, lanes] * phase_ref[source, 0:1, lanes]
                + base_buf[1, :, lanes] * phase_ref[source, 1:2, lanes]
            ).astype(jnp.bfloat16)
            value = jnp.dot(rows, table, preferred_element_type=jnp.float32)
            total[j] = value if first else total[j] + value

    accumulate(blocks_ref[me], me, True)

    def receive(t, carry):
        arrival(t).wait_recv()
        source = flip(me, t, col_total)
        accumulate(landed[source], source, False)
        return carry

    lax.fori_loop(1, col_total, receive, 0)

    def band_copy(j, to_peer):
        peer = (band + j) % band_total
        return pltpu.make_async_remote_copy(
            src_ref=outgoing.at[peer],
            dst_ref=incoming.at[band if to_peer else peer],
            send_sem=band_send.at[peer],
            recv_sem=band_recv.at[band if to_peer else peer],
            device_id={"band": peer},
            device_id_type=MESH,
        )

    for j in range(1, band_total):
        peer = (band + j) % band_total
        outgoing[peer] = total[peer].astype(jnp.bfloat16)
    for j in range(1, band_total):
        band_copy(j, True).start()
    shape = (level_total, row_total, piece_width)
    out_ref[:, band] = total[band].reshape(shape)
    for j in range(1, band_total):
        peer = (band + j) % band_total
        band_copy(j, False).wait_recv()
        out_ref[:, peer] = incoming[peer].astype(jnp.float32).reshape(shape)

    def drain(t, carry):
        block_copy(t).wait_send()
        return carry

    lax.fori_loop(1, col_total, drain, 0)
    for j in range(1, band_total):
        band_copy(j, True).wait_send()


def tables(width, col_total, band_total):
    length = width * col_total
    waves = np.arange(length // 4, dtype=np.int64).reshape(band_total, 1, -1)
    wave_of = np.broadcast_to(waves, (band_total, 2, waves.shape[-1])).reshape(-1)
    imaginary = np.broadcast_to(np.arange(2).reshape(1, 2, 1), (band_total, 2, waves.shape[-1])).reshape(-1)
    angle = 2.0 * np.pi * ((np.arange(width)[:, None] * wave_of[None, :]) % length) / length
    cosine, sine = np.cos(angle), np.sin(angle)
    plain = np.where(imaginary[None, :] == 1, -sine, cosine)
    crossed = np.where(imaginary[None, :] == 1, -cosine, -sine)
    base = np.stack([plain, crossed]) / math.sqrt(length)
    turn = 2.0 * np.pi * ((np.arange(col_total)[:, None] * wave_of[None, :]) % col_total) / col_total
    phase = np.stack([np.cos(turn), np.sin(turn)], axis=1)
    return base.astype(np.float32), phase.astype(np.float32)


def shards(fields, inverse, block_costs, row_length):
    field_total, level_total, row_total, width = fields.shape
    col_total, band_total = lax.axis_size("col"), lax.axis_size("band")
    own_levels = field_total * level_total // col_total
    vmem = pl.BlockSpec(memory_space=pltpu.VMEM)
    smem = pl.BlockSpec(memory_space=pltpu.SMEM)
    masked = pl.pallas_call(
        relax_kernel,
        name="relax",
        out_shape=jax.ShapeDtypeStruct(fields.shape, jnp.bfloat16),
        in_specs=[smem, smem, vmem, vmem],
        out_specs=vmem,
        scratch_shapes=[
            pltpu.VMEM((field_total, level_total, row_total * width), jnp.bfloat16),
            pltpu.VMEM((field_total, level_total, row_total * width), jnp.bfloat16),
            pltpu.VMEM((field_total, level_total * row_total, width), jnp.float32),
        ],
    )(block_costs, row_length, fields, inverse)
    blocks = masked.reshape(col_total, own_levels, row_total, width)
    base, phase = tables(width, col_total, band_total)
    own_rows, piece_width = own_levels * row_total, base.shape[2] // band_total
    spectra = pl.pallas_call(
        functools.partial(fourier_kernel, col_total, band_total),
        name="fourier",
        out_shape=jax.ShapeDtypeStruct((own_levels, band_total, row_total, piece_width), jnp.float32),
        in_specs=[vmem, pl.BlockSpec(memory_space=pl.ANY), vmem],
        out_specs=vmem,
        scratch_shapes=[
            pltpu.VMEM((col_total, own_levels, row_total, width), jnp.bfloat16),
            pltpu.VMEM((band_total, own_rows, piece_width), jnp.float32),
            pltpu.VMEM((band_total, own_rows, piece_width), jnp.bfloat16),
            pltpu.VMEM((band_total, own_rows, piece_width), jnp.bfloat16),
            pltpu.VMEM(base.shape, jnp.float32),
            pltpu.SemaphoreType.DMA((col_total,)),
            pltpu.SemaphoreType.DMA((col_total,)),
            pltpu.SemaphoreType.DMA((band_total,)),
            pltpu.SemaphoreType.DMA((band_total,)),
            pltpu.SemaphoreType.DMA,
        ],
        compiler_params=pltpu.CompilerParams(collective_id=0, has_side_effects=True),
    )(blocks, jnp.asarray(base), jnp.asarray(phase))
    return spectra.reshape(own_levels, band_total * row_total, 2, piece_width // 2)


def solution(mesh):
    return jax.shard_map(
        shards,
        mesh=mesh,
        in_specs=(P(None, None, "band", "col"), P(), P("col", "band"), P("band")),
        out_specs=P("col", None, None, "band"),
        check_vma=False,
    )
```

time: 90.5 us -> 40.4 us (0.45)
  Pallas kernels: 0 us -> 37.9 us
  local copies, waits for them, and re-layouts: 26.6 us -> 2.33 us
  waiting for transfers between devices: 16.2 us -> 0 us
  starting transfers between devices: 13.3 us -> 0 us
  blocking collectives: 12.4 us -> 0 us
  loops' own time: 7.9 us -> 0 us
  matrix products: 6.9 us -> 0 us
  other arithmetic: 6.54 us -> 0 us
    pallas_call x0 -> x2, Pallas kernels: none -> 37.9 us  [the longest x1 32.5 us: shards(): pl.pallas_call(functools.partial(fourier_kernel, col_total, band_total),...]
    all_to_all x1 -> x0, waiting for transfers between devices: 16.2 us -> none  [shards(): lax.all_to_all(flat_blocks, 'col', split_axis=0, concat_axis=2, tiled=True)]
    unnamed x11 -> x0, local copies, waits for them, and re-layouts: 14.7 us -> none
    all_to_all x1 -> x0, starting transfers between devices: 13.3 us -> none  [shards(): lax.all_to_all(flat_blocks, 'col', split_axis=0, concat_axis=2, tiled=True)]
    all_to_all x1 -> x0, blocking collectives: 12.4 us -> none  [shards(): lax.all_to_all(rows_fourier, 'band', split_axis=3, concat_axis=1, tiled=T...]
    another operation x3 -> x0, loops' own time: 7.9 us -> none  [the longest x2 7.82 us: one_group(): lax.fori_loop(jnp.int32(0), jnp.max(steps_here), sweep, block_set)]
    dot_general x11 -> x0, matrix products: 6.9 us -> none  [the longest x1 3.63 us: transform(): jnp.einsum('iprmb,iboq->proqm', twisted, table_two, precision=lax.Precisi...]
    all_to_all x4 -> x0, local copies, waits for them, and re-layouts: 5.65 us -> none  [shards(): lax.all_to_all(rows_fourier, 'band', split_axis=3, concat_axis=1, tiled=T...]
  transfers between devices with their start and end apart: 1 -> 0, of which waited for: 1 -> 0; matrix products, arithmetic and copies ran while one was open for 0% -> 0% of each run, Pallas kernels for 0% -> 0%
where the time goes in v1:
time: 40.4 us; the launch traced here: 40.2 us
  Pallas kernels  37.9 us (94%)
  local copies, waits for them, and re-layouts  2.33 us (6%)
    pallas_call x1, Pallas kernels, shards(): pl.pallas_call(functools.partial(fourier_kernel, col_total, band_total),...  32.5 us
    pallas_call x1, Pallas kernels, shards(): pl.pallas_call(relax_kernel, name='relax', out_shape=jax.ShapeDtypeStruct...  5.38 us
    reshape x1, local copies, waits for them, and re-layouts, shards(): spectra.reshape(own_levels, band_total * row_total, 2, piece_width // 2)  2.33 us

profile of v1, /device:TPU:0, one launch (start us, length us, event | category | flops | bytes accessed | tf_op | source)
XLA Modules:
  0.0 40.2 jit_solution(2972381526874836195)
XLA Ops:
  0.0 5.4 %relax.1 = bf16[4,80,8,128]{3,2,1,0:T(8,128)(2,1)} custom-call(s32[1,8]{1,0:T(1,128)} %cost_ref.1, s32[8]{0:T(128)} %length_ref.1, bf16[4,80,8,128]{3,2,1,0:T(8,128)(2,1)} %fields_ref.1, bf16[4,80,80]{2,1,0:T(8,128)(2,1)} %inverse_ref.1), custom_call_target="tpu_custom_call" | custom-call | tf_op jit(solution)/shard_map/relax/pallas_call | solution.py:189
  5.4 32.5 %fourier.1 = f32[20,2,8,512]{3,2,1,0:T(8,128)} custom-call(bf16[16,20,8,128]{3,2,1,0:T(8,128)(2,1)} %bitcast.3, f32[2,128,1024]{2,1,0:T(8,128)} %constant.4.clone.base_ref, f32[16,2,1024]{2,1,0:T(2,128)} %constant.5.clone.phase_ref), custom_call_target="tpu_custom_call" | custom-call | tf_op jit(solution)/shard_map/fourier/pallas_call | solution.py:204
  37.9 2.3 %reshape.7 = f32[20,16,2,256]{3,2,1,0:T(2,128)} reshape(f32[20,2,8,512]{3,2,1,0:T(8,128)} %fourier.1) | data formatting | bytes 1310720 | tf_op jit(solution)/shard_map/reshape | solution.py:224

commit v2 on v1

v2 whole, which is shorter than its diff:
```python
import functools
import math

import jax
import jax.numpy as jnp
import numpy as np
from jax import lax
from jax.experimental import pallas as pl
from jax.experimental.pallas import tpu as pltpu
from jax.sharding import PartitionSpec as P

sweep_total = 8
MESH = pl.DeviceIdType.MESH


def flip(position, step, total):
    result, bit = 0, 1
    while bit < total:
        result = result + bit * (((position // bit) + (step // bit)) % 2)
        bit *= 2
    return result


def spectral_kernel(
    col_total, band_total, scale,
    cost_ref, length_ref, fields_ref, inverse_ref, base_ref, phase_ref, out_ref,
    fields_buf, turn_in, turn_out, state_ref, blocks, landed, total, outgoing, incoming, base_buf,
    field_sem, base_sem, send_sem, recv_sem, band_send, band_recv,
):
    me, band = lax.axis_index("col"), lax.axis_index("band")
    field_total, level_total, row_total, width = fields_buf.shape
    own_levels = landed.shape[1]
    piece_width = total.shape[2]
    group = col_total // field_total
    place, inside = me // group, me % group
    toward = 1 - 2 * (place // (field_total // 2))
    head = (3 * own_levels + 4) // 5
    chunks = ((0, head), (head, own_levels - head))

    def field_of(i):
        return (place + field_total + toward * (1 + i)) % field_total

    def field_copy(i):
        f = field_of(i)
        return pltpu.make_async_copy(fields_ref.at[f], fields_buf.at[i], field_sem.at[i])

    for i in range(field_total):
        field_copy(i).start()
    base_copy = pltpu.make_async_copy(base_ref, base_buf, base_sem)
    base_copy.start()
    barrier = pltpu.get_barrier_semaphore()

    def greet(t, carry):
        pl.semaphore_signal(
            barrier, inc=1, device_id={"col": (me + t) % col_total}, device_id_type=MESH
        )
        return carry

    lax.fori_loop(1, col_total, greet, 0)
    for j in range(1, band_total):
        pl.semaphore_signal(
            barrier, inc=1, device_id={"band": (band + j) % band_total}, device_id_type=MESH
        )

    costs = jnp.concatenate(
        [jnp.full((1, width), cost_ref[0, r], jnp.int32) for r in range(row_total)], axis=1
    )
    longitude = me * width + lax.broadcasted_iota(jnp.int32, (1, width), 1)
    keep = jnp.concatenate(
        [(longitude < length_ref[r]).astype(jnp.int32) for r in range(row_total)], axis=0
    )[None] > 0

    def relax(pair):
        for k in range(2):
            field_copy(2 * pair + k).wait()
            turn_in[k] = (
                fields_buf[2 * pair + k].astype(jnp.float32).reshape(level_total * row_total, width)
            )
        for k in range(2):
            for r in range(row_total):
                piece = turn_in[k, pl.ds(r, level_total, stride=row_total), :]
                state_ref[k, :, r * width : (r + 1) * width] = piece.astype(jnp.bfloat16)

        def sweep(s, carry):
            active = costs > s
            for k in range(2):
                before = state_ref[k]
                applied = jnp.dot(
                    inverse_ref[field_of(2 * pair + k)], before, preferred_element_type=jnp.float32
                )
                state_ref[k] = jnp.where(
                    active, applied, before.astype(jnp.float32)
                ).astype(jnp.bfloat16)
            return carry

        lax.fori_loop(0, sweep_total, sweep, 0)
        for k in range(2):
            for r in range(row_total):
                turn_out[k, pl.ds(r, level_total, stride=row_total), :] = state_ref[
                    k, :, r * width : (r + 1) * width
                ].astype(jnp.float32)
        for k in range(2):
            f = field_of(2 * pair + k)
            for q in range(group):
                rows = slice(q * own_levels * row_total, (q + 1) * own_levels * row_total)
                shape = (own_levels, row_total, width)
                initial = turn_in[k, rows, :].reshape(shape)
                tendency = (turn_out[k, rows, :].reshape(shape) - initial).astype(jnp.bfloat16)
                updated = initial + tendency.astype(jnp.float32)
                blocks[f * group + q] = jnp.where(keep, updated, 0.0).astype(jnp.bfloat16)

    def block_copy(chunk, peer, source):
        start, size = chunks[chunk]
        return pltpu.make_async_remote_copy(
            src_ref=blocks.at[peer, pl.ds(start, size)],
            dst_ref=landed.at[source, pl.ds(start, size)],
            send_sem=send_sem.at[chunk, peer],
            recv_sem=recv_sem.at[chunk, source],
            device_id={"col": peer},
            device_id_type=MESH,
        )

    def send_field(chunk, i, first):
        for j in range(first, group):
            peer = field_of(i) * group + (inside + j) % group
            block_copy(chunk, peer, me).start()

    def send_pair(chunk, pair, last):
        for i in range(2):
            send_field(chunk, 2 * pair + i, 1 if last and i == 1 else 0)

    def relax_and_send(pair, carry):
        relax(pair)
        send_pair(0, pair, False)
        return carry

    relax(0)
    pl.semaphore_wait(barrier, col_total - 1 + band_total - 1)
    send_pair(0, 0, False)
    lax.fori_loop(1, field_total // 2 - 1, relax_and_send, 0)
    relax(field_total // 2 - 1)
    send_pair(0, field_total // 2 - 1, True)

    def second_chunk(i, carry):
        send_field(1, i, 0)
        return carry

    lax.fori_loop(0, field_total - 1, second_chunk, 0)
    send_field(1, field_total - 1, 1)
    base_copy.wait()

    def rows_of(ref, source, chunk):
        start, size = chunks[chunk]
        values = ref[source, start : start + size].astype(jnp.float32)
        return values.reshape(size * row_total, width).astype(jnp.bfloat16)

    def accumulate(chunk, first_rows, second_rows, sources, fresh):
        start, size = chunks[chunk]
        held = slice(start * row_total, (start + size) * row_total)
        rows = jnp.concatenate([first_rows, second_rows], axis=1)
        for j in range(band_total):
            lanes = slice(j * piece_width, (j + 1) * piece_width)
            table = jnp.concatenate(
                [
                    (
                        base_buf[0, :, lanes] * phase_ref[source, 0:1, lanes]
                        + base_buf[1, :, lanes] * phase_ref[source, 1:2, lanes]
                    ).astype(jnp.bfloat16)
                    for source in sources
                ],
                axis=0,
            )
            value = jnp.dot(rows, table, preferred_element_type=jnp.float32)
            total[j, held] = value if fresh else total[j, held] + value

    def band_copy(chunk, j, to_peer):
        start, size = chunks[chunk]
        held = pl.ds(start * row_total, size * row_total)
        peer = (band + j) % band_total
        origin = band if to_peer else peer
        return pltpu.make_async_remote_copy(
            src_ref=outgoing.at[chunk, peer, held],
            dst_ref=incoming.at[chunk, origin, held],
            send_sem=band_send.at[chunk, peer],
            recv_sem=band_recv.at[chunk, origin],
            device_id={"band": peer},
            device_id_type=MESH,
        )

    mate = me + 1 - 2 * (me % 2)
    for chunk, (start, size) in enumerate(chunks):
        held = slice(start * row_total, (start + size) * row_total)
        block_copy(chunk, mate, mate).wait_recv()
        accumulate(
            chunk, rows_of(blocks, me, chunk), rows_of(landed, mate, chunk), (me, mate), True
        )

        def receive(t, carry):
            first = 2 * flip(me // 2, t, col_total // 2)
            block_copy(chunk, first, first).wait_recv()
            block_copy(chunk, first + 1, first + 1).wait_recv()
            accumulate(
                chunk, rows_of(landed, first, chunk), rows_of(landed, first + 1, chunk),
                (first, first + 1), False,
            )
            return carry

        lax.fori_loop(1, col_total // 2, receive, 0)
        for j in range(1, band_total):
            peer = (band + j) % band_total
            outgoing[chunk, peer, held] = (total[peer, held] * scale).astype(jnp.bfloat16)
        for j in range(1, band_total):
            band_copy(chunk, j, True).start()

    def put(origin, start, size, values):
        pieces = piece_width // 128
        for level in range(size):
            rows = values[level * row_total : (level + 1) * row_total]
            for k in range(pieces):
                out_ref[start + level, origin, pl.ds(k, row_total, stride=pieces), :] = rows[
                    :, k * 128 : (k + 1) * 128
                ]

    for start, size in chunks:
        held = slice(start * row_total, (start + size) * row_total)
        put(band, start, size, total[band, held] * scale)
    for chunk, (start, size) in enumerate(chunks):
        held = slice(start * row_total, (start + size) * row_total)
        for j in range(1, band_total):
            peer = (band + j) % band_total
            band_copy(chunk, j, False).wait_recv()
            put(peer, start, size, incoming[chunk, peer, held].astype(jnp.float32))

    def drain(t, carry):
        peer = (me + t) % col_total
        for chunk in range(len(chunks)):
            block_copy(chunk, peer, me).wait_send()
        return carry

    lax.fori_loop(1, col_total, drain, 0)
    for chunk in range(len(chunks)):
        for j in range(1, band_total):
            band_copy(chunk, j, True).wait_send()


def tables(width, col_total, band_total):
    length = width * col_total
    waves = np.arange(length // 4, dtype=np.int64).reshape(-1, 1, 128)
    shape = (waves.shape[0], 2, 128)
    wave_of = np.broadcast_to(waves, shape).reshape(-1)
    imaginary = np.broadcast_to(np.arange(2).reshape(1, 2, 1), shape).reshape(-1)
    angle = 2.0 * np.pi * ((np.arange(width)[:, None] * wave_of[None, :]) % length) / length
    cosine, sine = np.cos(angle), np.sin(angle)
    plain = np.where(imaginary[None, :] == 1, -sine, cosine)
    crossed = np.where(imaginary[None, :] == 1, -cosine, -sine)
    base = np.stack([plain, crossed])
    turn = 2.0 * np.pi * ((np.arange(col_total)[:, None] * wave_of[None, :]) % col_total) / col_total
    phase = np.stack([np.cos(turn), np.sin(turn)], axis=1)
    return base.astype(np.float32), phase.astype(np.float32)


def shards(fields, inverse, block_costs, row_length):
    field_total, level_total, row_total, width = fields.shape
    col_total, band_total = lax.axis_size("col"), lax.axis_size("band")
    own_levels = field_total * level_total // col_total
    vmem = pl.BlockSpec(memory_space=pltpu.VMEM)
    smem = pl.BlockSpec(memory_space=pltpu.SMEM)
    hbm = pl.BlockSpec(memory_space=pl.ANY)
    base, phase = tables(width, col_total, band_total)
    own_rows, piece_width = own_levels * row_total, base.shape[2] // band_total
    waves = piece_width // 2
    spectra = pl.pallas_call(
        functools.partial(
            spectral_kernel, col_total, band_total, 1.0 / math.sqrt(width * col_total)
        ),
        name="spectral",
        out_shape=jax.ShapeDtypeStruct((own_levels, band_total, row_total * piece_width // 128, 128), jnp.float32),
        in_specs=[smem, smem, hbm, vmem, hbm, vmem],
        out_specs=vmem,
        scratch_shapes=[
            pltpu.VMEM(fields.shape, jnp.bfloat16),
            pltpu.VMEM((2, level_total * row_total, width), jnp.float32),
            pltpu.VMEM((2, level_total * row_total, width), jnp.float32),
            pltpu.VMEM((2, level_total, row_total * width), jnp.bfloat16),
            pltpu.VMEM((col_total, own_levels, row_total, width), jnp.bfloat16),
            pltpu.VMEM((col_total, own_levels, row_total, width), jnp.bfloat16),
            pltpu.VMEM((band_total, own_rows, piece_width), jnp.float32),
            pltpu.VMEM((2, band_total, own_rows, piece_width), jnp.bfloat16),
            pltpu.VMEM((2, band_total, own_rows, piece_width), jnp.bfloat16),
            pltpu.VMEM(base.shape, jnp.float32),
            pltpu.SemaphoreType.DMA((field_total,)),
            pltpu.SemaphoreType.DMA,
            pltpu.SemaphoreType.DMA((2, col_total)),
            pltpu.SemaphoreType.DMA((2, col_total)),
            pltpu.SemaphoreType.DMA((2, band_total)),
            pltpu.SemaphoreType.DMA((2, band_total)),
        ],
        compiler_params=pltpu.CompilerParams(collective_id=0, has_side_effects=True),
    )(block_costs, row_length, fields, inverse, jnp.asarray(base), jnp.asarray(phase))
    split = spectra.reshape(own_levels, band_total * row_total, waves // 128, 2, 128)
    return split.transpose(0, 1, 3, 2, 4).reshape(own_levels, band_total * row_total, 2, waves)


def solution(mesh):
    return jax.shard_map(
        shards,
        mesh=mesh,
        in_specs=(P(None, None, "band", "col"), P(), P("col", "band"), P("band")),
        out_specs=P("col", None, None, "band"),
        check_vma=False,
    )
```

time: 40.4 us -> 33.2 us (0.82)
  Pallas kernels: 37.9 us -> 30.7 us
    pallas_call x2 -> x1, Pallas kernels: 37.9 us -> 30.7 us  [shards(): pl.pallas_call(functools.partial(spectral_kernel, col_total, band_total,...]
    reshape x1 -> x0, local copies, waits for them, and re-layouts: 2.33 us -> none  [shards(): spectra.reshape(own_levels, band_total * row_total, 2, piece_width // 2)]
    unnamed x0 -> x1, local copies, waits for them, and re-layouts: none -> 2.25 us
where the time goes in v2:
time: 33.2 us; the launch traced here: 33 us
  Pallas kernels  30.7 us (92%)
  local copies, waits for them, and re-layouts  2.25 us (7%)
    pallas_call x1, Pallas kernels, shards(): pl.pallas_call(functools.partial(spectral_kernel, col_total, band_total,...  30.7 us
    unnamed x1, local copies, waits for them, and re-layouts  2.25 us

profile of v2, /device:TPU:0, one launch (start us, length us, event | category | flops | bytes accessed | tf_op | source)
XLA Modules:
  0.0 33.0 jit_solution(5739362205851758536)
XLA Ops:
  0.0 30.7 %spectral.1 = f32[20,2,32,128]{3,2,1,0:T(8,128)} custom-call(s32[1,8]{1,0:T(1,128)} %cost_ref.1, s32[8]{0:T(128)} %length_ref.1, bf16[4,80,8,128]{3,2,1,0:T(8,128)(2,1)} %fields_ref.1, bf16[4,80,80]{2,1,0:T(8,128)(2,1)} %inverse_ref.1, f32[2,128,1024]{2,1,0:T(8,128)} %constant.4.clone.base_ref, f32[16,2,1024]{2,1,0:T(2,128)} %constant.5.clone.phase_ref), custom_call_target="tpu_custom_call" | custom-call | tf_op jit(solution)/shard_map/spectral/pallas_call | solution.py:272
  30.7 2.2 %copy.9 = f32[20,16,2,256]{3,2,1,0:T(2,128)} copy(f32[20,16,2,256]{3,2,1,0:T(2,128)} %bitcast.5) | data formatting | bytes 1310720

commit v3 on v2

--- a/solution.py
+++ b/solution.py
@@ -241,6 +241,26 @@
     for chunk in range(len(chunks)):
         for j in range(1, band_total):
             band_copy(chunk, j, True).wait_send()
+
+
+def deliver_kernel(size, in_ref, out_ref, held, in_sem, out_sem):
+    pieces = held.shape[0] // size
+    parts = [pl.ds(p * size, size) for p in range(pieces)]
+    reads = [
+        pltpu.make_async_copy(in_ref.at[part], held.at[part], in_sem.at[p])
+        for p, part in enumerate(parts)
+    ]
+    writes = [
+        pltpu.make_async_copy(held.at[part], out_ref.at[part], out_sem.at[p])
+        for p, part in enumerate(parts)
+    ]
+    for read in reads:
+        read.start()
+    for read, write in zip(reads, writes):
+        read.wait()
+        write.start()
+    for write in writes:
+        write.wait()
 
 
 def tables(width, col_total, band_total):
@@ -297,6 +317,19 @@
         ],
         compiler_params=pltpu.CompilerParams(collective_id=0, has_side_effects=True),
     )(block_costs, row_length, fields, inverse, jnp.asarray(base), jnp.asarray(phase))
+    pieces = next(p for p in (5, 4, 2, 1) if own_levels % p == 0)
+    spectra = pl.pallas_call(
+        functools.partial(deliver_kernel, own_levels // pieces),
+        name="deliver",
+        out_shape=jax.ShapeDtypeStruct(spectra.shape, spectra.dtype),
+        in_specs=[hbm],
+        out_specs=hbm,
+        scratch_shapes=[
+            pltpu.VMEM(spectra.shape, spectra.dtype),
+            pltpu.SemaphoreType.DMA((pieces,)),
+            pltpu.SemaphoreType.DMA((pieces,)),
+        ],
+    )(spectra)
     split = spectra.reshape(own_levels, band_total * row_total, waves // 128, 2, 128)
     return split.transpose(0, 1, 3, 2, 4).reshape(own_levels, band_total * row_total, 2, waves)
 

time: 33.2 us -> 32.8 us (0.988)
  local copies, waits for them, and re-layouts: 2.25 us -> 0 us
  Pallas kernels: 30.7 us -> 32.6 us
    unnamed x1 -> x0, local copies, waits for them, and re-layouts: 2.25 us -> none
    pallas_call x0 -> x1, Pallas kernels: none -> 1.91 us  [shards(): pl.pallas_call(functools.partial(deliver_kernel, own_levels // pieces), n...]
where the time goes in v3:
time: 32.8 us; the launch traced here: 32.6 us
  Pallas kernels  32.6 us (99%)
    pallas_call x1, Pallas kernels, shards(): pl.pallas_call(functools.partial(spectral_kernel, col_total, band_total,...  30.7 us
    pallas_call x1, Pallas kernels, shards(): pl.pallas_call(functools.partial(deliver_kernel, own_levels // pieces), n...  1.91 us

profile of v3, /device:TPU:0, one launch (start us, length us, event | category | flops | bytes accessed | tf_op | source)
XLA Modules:
  0.0 32.6 jit_solution(13877297402295984512)
XLA Ops:
  0.0 30.7 %spectral.1.in_ref = f32[20,2,32,128]{3,2,1,0:T(8,128)} custom-call(s32[1,8]{1,0:T(1,128)} %cost_ref.1, s32[8]{0:T(128)} %length_ref.1, bf16[4,80,8,128]{3,2,1,0:T(8,128)(2,1)} %fields_ref.1, bf16[4,80,80]{2,1,0:T(8,128)(2,1)} %inverse_ref.1, f32[2,128,1024]{2,1,0:T(8,128)} %constant.4.clone.base_ref, f32[16,2,1024]{2,1,0:T(2,128)} %constant.5.clone.phase_ref), custom_call_target="tpu_custom_call" | custom-call | tf_op jit(solution)/shard_map/spectral/pallas_call | solution.py:292
  30.7 1.9 %deliver.1 = f32[20,2,32,128]{3,2,1,0:T(8,128)} custom-call(f32[20,2,32,128]{3,2,1,0:T(8,128)} %spectral.1.in_ref), custom_call_target="tpu_custom_call" | custom-call | tf_op jit(solution)/shard_map/deliver/pallas_call | solution.py:321

commit v4 on v3

--- a/solution.py
+++ b/solution.py
@@ -93,7 +93,7 @@
                 ).astype(jnp.bfloat16)
             return carry
 
-        lax.fori_loop(0, sweep_total, sweep, 0)
+        lax.fori_loop(0, sweep_total, sweep, 0, unroll=True)
         for k in range(2):
             for r in range(row_total):
                 turn_out[k, pl.ds(r, level_total, stride=row_total), :] = state_ref[

time: 32.8 us -> 32.3 us (0.985)
  Pallas kernels: 32.6 us -> 32.1 us
    pallas_call x1, Pallas kernels: 30.7 us -> 30.2 us  [shards(): pl.pallas_call(functools.partial(spectral_kernel, col_total, band_total,...]
where the time goes in v4:
time: 32.3 us; the launch traced here: 32.1 us
  Pallas kernels  32.1 us (99%)
    pallas_call x1, Pallas kernels, shards(): pl.pallas_call(functools.partial(spectral_kernel, col_total, band_total,...  30.2 us
    pallas_call x1, Pallas kernels, shards(): pl.pallas_call(functools.partial(deliver_kernel, own_levels // pieces), n...  1.91 us

profile of v4, /device:TPU:0, one launch (start us, length us, event | category | flops | bytes accessed | tf_op | source)
XLA Modules:
  0.0 32.1 jit_solution(7747051889259195114)
XLA Ops:
  0.0 30.2 %spectral.1.in_ref = f32[20,2,32,128]{3,2,1,0:T(8,128)} custom-call(s32[1,8]{1,0:T(1,128)} %cost_ref.1, s32[8]{0:T(128)} %length_ref.1, bf16[4,80,8,128]{3,2,1,0:T(8,128)(2,1)} %fields_ref.1, bf16[4,80,80]{2,1,0:T(8,128)(2,1)} %inverse_ref.1, f32[2,128,1024]{2,1,0:T(8,128)} %constant.4.clone.base_ref, f32[16,2,1024]{2,1,0:T(2,128)} %constant.5.clone.phase_ref), custom_call_target="tpu_custom_call" | custom-call | tf_op jit(solution)/shard_map/spectral/pallas_call | solution.py:292
  30.2 1.9 %deliver.1 = f32[20,2,32,128]{3,2,1,0:T(8,128)} custom-call(f32[20,2,32,128]{3,2,1,0:T(8,128)} %spectral.1.in_ref), custom_call_target="tpu_custom_call" | custom-call | tf_op jit(solution)/shard_map/deliver/pallas_call | solution.py:321
